TPU v7x, 32 devices: a whole 2x2x4 slice. The times are simulated.
32 devices in a mesh: team: 2 (over x), blk: 4 (over z), head: 4 (over y, core).
Axes of the slice: x: 2, y: 2, z: 4, core: 2. Of those that a mesh axis runs over, the one named last changes fastest.
Arguments:
- queries: bfloat16 [1024, 8, 8, 128], P('blk', 'head', 'team'), may hold values from -40 to 40
- features: bfloat16 [1024, 8192], P('blk', ('team', 'head')), may hold values from -6 to 6
- adapter_down: bfloat16 [4, 8192, 64], P(None, ('team', 'head')), may hold values from -0.0625 to 0.0625
- adapter_key_up: bfloat16 [4, 64, 8, 128], P(None, None, 'head'), may hold values from -0.75 to 0.75
- adapter_value_up: bfloat16 [4, 64, 8, 128], P(None, None, 'head'), may hold values from -0.75 to 0.75
- base_key: bfloat16 [1024, 8, 128], P('blk', 'head'), may hold values from -6 to 6
- base_value: bfloat16 [1024, 8, 128], P('blk', 'head'), may hold values from -24 to 24
- prefix_key: bfloat16 [2048, 8, 128], P('blk', 'head'), may hold values from -7 to 7
- prefix_value: bfloat16 [2048, 8, 128], P('blk', 'head'), may hold values from -24 to 24
- adapter_ids: int32 [4], replicated, may hold values from 0 to 3
- block_order: int32 [4], replicated, may hold values from 0 to 15
Outputs:
- attended: bfloat16 [1024, 8, 8, 128], P('blk', 'head', 'team')
All inputs are finite; a program needn't handle non-finite values.
Results may differ from a plain program's by a relative error of at most 0.011.
Values may be sent and summed in bfloat16 or wider, within the bound.
No kernel may reach another device: no remote copies, remote signals or barrier semaphores. Data moves between devices by JAX's collectives and lax.ppermute only.
A program may use at most 64 MiB of HBM per device.

v0:
```python
import math
import jax
import jax.numpy as jnp
from jax import lax
from jax.sharding import PartitionSpec as P

NEG_FILL = -1e30


def block_length(row_count):
    for candidate in range(min(row_count, 1024), 0, -1):
        if row_count % candidate == 0:
            return candidate
    return row_count


def key_positions(row_count, shard_rows, prefix_dev, query_dev, block_order, block_count):
    row_index = jnp.arange(row_count, dtype=jnp.int32)
    holder = row_index // shard_rows
    within = row_index - holder * shard_rows
    block_ids = jnp.arange(block_count, dtype=jnp.int32)
    holder_order = jnp.sum(
        jnp.where(holder[:, None] == block_ids[None, :], block_order[None, :], 0), axis=1
    )
    later = prefix_dev * block_count + holder_order * query_dev + within - prefix_dev
    return jnp.where(within < prefix_dev, holder * prefix_dev + within, later)


def attend(running, query_rows, query_pos, key_rows, value_rows, key_pos):
    row_count = key_rows.shape[0]
    block_rows = block_length(row_count)
    key_blocks = row_count // block_rows
    kv_heads = key_rows.shape[1]
    head_dim = key_rows.shape[2]
    score_scale = 1.0 / math.sqrt(head_dim)
    latest = jnp.max(query_pos)
    key_split = key_rows.reshape((key_blocks, block_rows, kv_heads, head_dim))
    value_split = value_rows.reshape((key_blocks, block_rows, kv_heads, head_dim))
    pos_split = key_pos.reshape((key_blocks, block_rows))

    def advance(carried, block_data):
        block_keys, block_values, block_pos = block_data

        def compute(previous):
            row_max, row_sum, weighted = previous
            scores = (
                jnp.einsum(
                    "tkgd,skd->kgts", query_rows, block_keys, preferred_element_type=jnp.float32
                )
                * score_scale
            )
            visible = block_pos[None, None, None, :] <= query_pos[None, None, :, None]
            scores = jnp.where(visible, scores, NEG_FILL)
            new_max = jnp.maximum(row_max, jnp.max(scores, axis=-1))
            weights = jnp.where(visible, jnp.exp(scores - new_max[..., None]), 0.0)
            factor = jnp.exp(row_max - new_max)
            row_sum = row_sum * factor + jnp.sum(weights, axis=-1)
            product = jnp.einsum(
                "kgts,skd->kgtd",
                weights.astype(jnp.bfloat16),
                block_values,
                preferred_element_type=jnp.float32,
            )
            weighted = weighted * factor[..., None] + product
            return (new_max, row_sum, weighted)

        return (lax.cond(jnp.min(block_pos) > latest, lambda kept: kept, compute, carried), None)

    result, _ = lax.scan(advance, running, (key_split, value_split, pos_split))
    return result


def on_device(
    queries,
    features,
    adapter_down,
    adapter_key_up,
    adapter_value_up,
    base_key,
    base_value,
    prefix_key,
    prefix_value,
    adapter_ids,
    block_order,
):
    block_count = lax.axis_size("blk")
    my_block = lax.axis_index("blk")
    query_dev = queries.shape[0]
    kv_heads = queries.shape[1]
    group_dev = queries.shape[2]
    head_dim = queries.shape[3]
    prefix_dev = prefix_key.shape[0]
    rank_width = adapter_down.shape[2]
    shard_rows = prefix_dev + query_dev
    chosen = adapter_ids[my_block]
    down_rows = lax.dynamic_index_in_dim(adapter_down, chosen, 0, keepdims=False)
    partial_latent = jnp.dot(features, down_rows, preferred_element_type=jnp.float32)
    latent = lax.psum(partial_latent, ("team", "head")).astype(jnp.bfloat16)

    def expand(up_table, base_rows):
        up_rows = lax.dynamic_index_in_dim(up_table, chosen, 0, keepdims=False).reshape(
            rank_width, kv_heads * head_dim
        )
        delta = jnp.dot(latent, up_rows, preferred_element_type=jnp.float32).reshape(
            query_dev, kv_heads, head_dim
        )
        return (base_rows.astype(jnp.float32) + delta).astype(jnp.bfloat16)

    key_rows = jnp.concatenate([prefix_key, expand(adapter_key_up, base_key)], axis=0)
    value_rows = jnp.concatenate([prefix_value, expand(adapter_value_up, base_value)], axis=0)
    prefix_total = prefix_dev * block_count
    offsets = jnp.arange(query_dev, dtype=jnp.int32)
    query_pos = prefix_total + block_order[my_block] * query_dev + offsets
    initial = (
        jnp.full((kv_heads, group_dev, query_dev), NEG_FILL, jnp.float32),
        jnp.zeros((kv_heads, group_dev, query_dev), jnp.float32),
        jnp.zeros((kv_heads, group_dev, query_dev, head_dim), jnp.float32),
    )
    key_piece = lax.all_gather(key_rows, "blk", axis=0, tiled=True)
    value_piece = lax.all_gather(value_rows, "blk", axis=0, tiled=True)
    piece_pos = key_positions(
        key_piece.shape[0], shard_rows, prefix_dev, query_dev, block_order, block_count
    )
    row_max, row_sum, weighted = attend(
        initial, queries, query_pos, key_piece, value_piece, piece_pos
    )
    result = weighted / row_sum[..., None]
    return result.transpose(2, 0, 1, 3).astype(jnp.bfloat16)


def solution(mesh):
    placed = (
        P("blk", "head", "team", None),
        P("blk", ("team", "head")),
        P(None, ("team", "head"), None),
        P(None, None, "head", None),
        P(None, None, "head", None),
        P("blk", "head", None),
        P("blk", "head", None),
        P("blk", "head", None),
        P("blk", "head", None),
        P(),
        P(),
    )
    return jax.shard_map(
        on_device,
        mesh=mesh,
        in_specs=placed,
        out_specs=P("blk", "head", "team", None),
        check_vma=False,
    )
```

profile of v0, /device:TPU:0, one launch (start us, length us, event | category | flops | bytes accessed | tf_op | source)
XLA Modules:
  0.0 160.4 jit_solution(10820601032562232662)
XLA Ops:
  6.5 1.3 dynamic_slice.39
  9.8 1.2 convolution_bitcast_fusion
  11.0 26.0 %psum.7 = bf16[256,64]{0,1:T(8,128)(2,1)S(1)} all-reduce(f32[256,64]{0,1:T(8,128)S(1)} %convolution_bitcast_fusion), channel_id=1, replica_groups=mesh['team'=2,'blk'=4,'head'=4] {'team','head'}, use_global_device_ids=true, to_apply=%region_0.1 | all-reduce | flops 16384 | bytes 98304 | tf_op jit(solution)/shard_map/psum | solution.py:98
  37.0 1.0 copy.35
  38.0 0.8 constant_dynamic-slice_fusion.1
  38.8 1.1 fusion.21
  39.9 0.8 pad_maximum_fusion
  40.7 0.0 all-gather.3.cloned.1.call-update
  40.7 0.0 all-gather.5.cloned.1.call-start
  40.8 1.0 copy.38
  41.8 1.1 fusion.22
  42.9 0.8 pad_maximum_fusion.1
  43.6 0.0 all-gather.5.cloned.1.call-update
  43.7 1.2 dynamic_slice.38
  45.5 0.6 add_reduce_fusion
  46.1 1.1 copy.40
  47.2 0.8 select_reduce_fusion
  48.1 29.3 %all-gather.3.cloned.1.call-done = bf16[3072,2,128]{2,0,1:T(8,128)(2,1)} async-done(((bf16[768,2,128]{2,0,1:T(8,128)(2,1)}), bf16[3072,2,128]{2,0,1:T(8,128)(2,1)}) %all-gather.3.cloned.1.call-update) | async-done | bytes 1572880 | tf_op jit(solution)/shard_map/all_gather | solution.py:119
  77.4 1.5 copy.39
  78.9 36.0 %all-gather.5.cloned.1.call-done = bf16[3072,2,128]{2,0,1:T(8,128)(2,1)} async-done(((bf16[768,2,128]{2,0,1:T(8,128)(2,1)}), bf16[3072,2,128]{2,0,1:T(8,128)(2,1)}) %all-gather.5.cloned.1.call-update) | async-done | bytes 1572880 | tf_op jit(solution)/shard_map/all_gather | solution.py:120
  114.9 2.7 %copy.41 = bf16[3,1024,2,128]{3,1,2,0:T(8,128)(2,1)} copy(bf16[3,1024,2,128]{3,1,0,2:T(8,128)(2,1)} %bitcast.83) | data formatting | bytes 3145728
  117.6 1.0 broadcast_in_dim.56
  118.6 31.8 %while.15 = (s32[]{:T(128)}, f32[2,4,256]{2,1,0:T(4,128)S(1)}, f32[2,4,256]{2,1,0:T(4,128)S(1)}, f32[2,4,256,128]{3,2,1,0:T(8,128)}, s32[3,1024]{1,0:T(4,128)S(1...) while((s32[]{:T(128)}, f32[2,4,256]{2,1,0:T(4,128)S(1)}, ...), condition=%wide.region_9.10_spmd.clone, body=%wide.region_3.9_spmd.clone.sunk | while | flops 1101796608 | bytes 38421312 | solution.py:69
  118.6 0.6 fusion.45
  120.5 8.7 %conditional.3 = (f32[2,4,256]{2,1,0:T(4,128)S(1)}, f32[2,4,256]{2,1,0:T(4,128)S(1)}, f32[2,4,256,128]{3,2,1,0:T(8,128)}) conditional(s32[]{:T(128)} %convert_element_type.57, (s32[1,1024]{1,0:T(1,128)S(1)}, s32[]{:T(128)}, bf16[3,1024,2,128]{3,1,2,0:T(8,128)(2,1)S(1)}, s32[]{:T(128)}, bf16[256,2,4,128]{3,0,2,1:T(8,128)(2,1)S(1)}, ...), branch_computations={%region_5.7_spmd, %region_8.8_spmd} | conditional | flops 1101795584 | bytes 38395480 | solution.py:67
  120.5 0.2 broadcast_compare_fusion
  120.7 0.0 copy-start.1
  120.7 1.4 fusion.2
  122.2 2.0 %fusion.4 = f32[2,4,256]{2,1,0:T(4,128)S(1)} fusion(f32[2,1024,256,4]{2,1,3,0:T(8,128)S(1)} %get-tuple-element.228, f32[2,4,256]{2,1,0:T(4,128)S(1)} %max.4, pred[256,1024]{0,1:T(8,128)(4,1)S(1)} %broadcast_compare_fusion), kind=kLoop, calls=%fused_computation.5 | loop fusion | flops 10483712 | bytes 8667136 | tf_op jit(solution)/shard_map/while/body/eval_jaxpr/cond/branch_0_fun/reduce_sum | solution.py:57
  124.2 4.0 %fusion.8 = f32[2,4,256,128]{3,2,1,0:T(8,128)S(1)} fusion(f32[2,1024,256,4]{2,1,3,0:T(8,128)S(1)} %get-tuple-element.228, f32[2,4,256]{2,1,0:T(4,128)S(1)} %max.4, pred[256,1024]{0,1:T(8,128)(4,1)S(1)} %broadcast_compare_fusion, f32[2,4,256,128]{3,2,1,0:T(8,128)S(1)} %copy-done.1, bf16[3,1024,2,128]{3,1,2,0:T(8,128)(2,1)} %get-tuple-element.125, ...), kind=kOutput, calls=%fused_computation.8 | convolution fusion | flops 547880960 | bytes 11289088 | tf_op jit(solution)/shard_map/while/body/eval_jaxpr/cond/branch_0_fun/kgts,skd->kgtd/dot_general | solution.py:58
  128.3 1.0 copy-done.2
  129.2 0.6 fusion.45
  131.1 8.7 %conditional.3 = (f32[2,4,256]{2,1,0:T(4,128)S(1)}, f32[2,4,256]{2,1,0:T(4,128)S(1)}, f32[2,4,256,128]{3,2,1,0:T(8,128)}) conditional(s32[]{:T(128)} %convert_element_type.57, (s32[1,1024]{1,0:T(1,128)S(1)}, s32[]{:T(128)}, bf16[3,1024,2,128]{3,1,2,0:T(8,128)(2,1)S(1)}, s32[]{:T(128)}, bf16[256,2,4,128]{3,0,2,1:T(8,128)(2,1)S(1)}, ...), branch_computations={%region_5.7_spmd, %region_8.8_spmd} | conditional | flops 1101795584 | bytes 38395480 | solution.py:67
  131.1 0.2 broadcast_compare_fusion
  131.3 0.0 copy-start.1
  131.3 1.4 fusion.2
  132.8 2.0 %fusion.4 = f32[2,4,256]{2,1,0:T(4,128)S(1)} fusion(f32[2,1024,256,4]{2,1,3,0:T(8,128)S(1)} %get-tuple-element.228, f32[2,4,256]{2,1,0:T(4,128)S(1)} %max.4, pred[256,1024]{0,1:T(8,128)(4,1)S(1)} %broadcast_compare_fusion), kind=kLoop, calls=%fused_computation.5 | loop fusion | flops 10483712 | bytes 8667136 | tf_op jit(solution)/shard_map/while/body/eval_jaxpr/cond/branch_0_fun/reduce_sum | solution.py:57
  134.8 4.0 %fusion.8 = f32[2,4,256,128]{3,2,1,0:T(8,128)S(1)} fusion(f32[2,1024,256,4]{2,1,3,0:T(8,128)S(1)} %get-tuple-element.228, f32[2,4,256]{2,1,0:T(4,128)S(1)} %max.4, pred[256,1024]{0,1:T(8,128)(4,1)S(1)} %broadcast_compare_fusion, f32[2,4,256,128]{3,2,1,0:T(8,128)S(1)} %copy-done.1, bf16[3,1024,2,128]{3,1,2,0:T(8,128)(2,1)} %get-tuple-element.125, ...), kind=kOutput, calls=%fused_computation.8 | convolution fusion | flops 547880960 | bytes 11289088 | tf_op jit(solution)/shard_map/while/body/eval_jaxpr/cond/branch_0_fun/kgts,skd->kgtd/dot_general | solution.py:58
  138.9 1.0 copy-done.2
  139.8 0.6 fusion.45
  141.7 8.7 %conditional.3 = (f32[2,4,256]{2,1,0:T(4,128)S(1)}, f32[2,4,256]{2,1,0:T(4,128)S(1)}, f32[2,4,256,128]{3,2,1,0:T(8,128)}) conditional(s32[]{:T(128)} %convert_element_type.57, (s32[1,1024]{1,0:T(1,128)S(1)}, s32[]{:T(128)}, bf16[3,1024,2,128]{3,1,2,0:T(8,128)(2,1)S(1)}, s32[]{:T(128)}, bf16[256,2,4,128]{3,0,2,1:T(8,128)(2,1)S(1)}, ...), branch_computations={%region_5.7_spmd, %region_8.8_spmd} | conditional | flops 1101795584 | bytes 38395480 | solution.py:67
  141.7 0.2 broadcast_compare_fusion
  141.9 1.4 fusion.2
  143.4 2.0 %fusion.4 = f32[2,4,256]{2,1,0:T(4,128)S(1)} fusion(f32[2,1024,256,4]{2,1,3,0:T(8,128)S(1)} %get-tuple-element.228, f32[2,4,256]{2,1,0:T(4,128)S(1)} %max.4, pred[256,1024]{0,1:T(8,128)(4,1)S(1)} %broadcast_compare_fusion), kind=kLoop, calls=%fused_computation.5 | loop fusion | flops 10483712 | bytes 8667136 | tf_op jit(solution)/shard_map/while/body/eval_jaxpr/cond/branch_0_fun/reduce_sum | solution.py:57
  145.4 4.0 %fusion.8 = f32[2,4,256,128]{3,2,1,0:T(8,128)S(1)} fusion(f32[2,1024,256,4]{2,1,3,0:T(8,128)S(1)} %get-tuple-element.228, f32[2,4,256]{2,1,0:T(4,128)S(1)} %max.4, pred[256,1024]{0,1:T(8,128)(4,1)S(1)} %broadcast_compare_fusion, f32[2,4,256,128]{3,2,1,0:T(8,128)S(1)} %copy-done.1, bf16[3,1024,2,128]{3,1,2,0:T(8,128)(2,1)} %get-tuple-element.125, ...), kind=kOutput, calls=%fused_computation.8 | convolution fusion | flops 547880960 | bytes 11289088 | tf_op jit(solution)/shard_map/while/body/eval_jaxpr/cond/branch_0_fun/kgts,skd->kgtd/dot_general | solution.py:58
  149.5 1.0 copy-done.2
  150.4 0.2 copy.42
  150.6 2.9 %fusion.24 = bf16[256,2,4,128]{3,2,1,0:T(4,128)(2,1)} fusion(f32[2,4,256]{1,0,2:T(2,128)S(1)} %copy.42, f32[2,4,256,128]{3,2,1,0:T(8,128)} %get-tuple-element.142), kind=kLoop, calls=%fused_computation.31 | loop fusion | flops 524288 | bytes 1581056 | tf_op jit(solution)/shard_map/convert_element_type | solution.py:128
  (31 shorter events, 0.2 us)
Async XLA Ops:
  6.5 3.2 %copy-start = (bf16[256,1024]{1,0:T(8,128)(2,1)S(1)}, bf16[256,1024]{1,0:T(8,128)(2,1)}, u32[]{:S(2)}) copy-start(bf16[256,1024]{1,0:T(8,128)(2,1)} %param.16) | copy-start | bytes 1572868
  6.5 70.8 %all-gather.3.cloned.1.call-start = ((), (), s32[]{:S(2)}) async-start(), calls=%async_computation | async-start | bytes 1966080 | tf_op jit(solution)/shard_map/all_gather | solution.py:119
  40.7 74.2 %all-gather.5.cloned.1.call-start = ((), (), s32[]{:S(2)}) async-start(), calls=%async_computation.1 | async-start | bytes 1966080 | tf_op jit(solution)/shard_map/all_gather | solution.py:120
  120.7 3.5 %copy-start.1 = (f32[2,4,256,128]{3,2,1,0:T(8,128)S(1)}, f32[2,4,256,128]{3,2,1,0:T(8,128)}, u32[]{:S(2)}) copy-start(f32[2,4,256,128]{3,2,1,0:T(8,128)} %get-tuple-element.124) | copy-start | bytes 3145732 | tf_op jit(solution)/shard_map/while/body/eval_jaxpr/cond
  128.3 1.0 copy-start.2
  131.3 3.5 %copy-start.1 = (f32[2,4,256,128]{3,2,1,0:T(8,128)S(1)}, f32[2,4,256,128]{3,2,1,0:T(8,128)}, u32[]{:S(2)}) copy-start(f32[2,4,256,128]{3,2,1,0:T(8,128)} %get-tuple-element.124) | copy-start | bytes 3145732 | tf_op jit(solution)/shard_map/while/body/eval_jaxpr/cond
  138.9 1.0 copy-start.2
  141.9 3.5 %copy-start.1 = (f32[2,4,256,128]{3,2,1,0:T(8,128)S(1)}, f32[2,4,256,128]{3,2,1,0:T(8,128)}, u32[]{:S(2)}) copy-start(f32[2,4,256,128]{3,2,1,0:T(8,128)} %get-tuple-element.124) | copy-start | bytes 3145732 | tf_op jit(solution)/shard_map/while/body/eval_jaxpr/cond
  149.5 1.0 copy-start.2
Sparse Core Ops, SparseCore 0:
  40.8 36.4 all-gather.2
  78.9 35.9 all-gather.4
where the time goes:
time: 161 us; the launch traced here: 160 us
  waiting for transfers between devices  65.4 us (41%)
  blocking collectives  26 us (16%)
  matrix products  19.7 us (12%)
  between operations  16 us (10%)
  local copies, waits for them, and re-layouts  14.8 us (9%)
  other arithmetic  14.6 us (9%)
  loops' own time  3.9 us (2%)
    all_gather x1, waiting for transfers between devices, on_device(): value_piece = lax.all_gather(value_rows, 'blk', axis=0, tiled=True)  36 us
    all_gather x1, waiting for transfers between devices, on_device(): key_piece = lax.all_gather(key_rows, 'blk', axis=0, tiled=True)  29.3 us
    psum x1, blocking collectives, on_device(): latent = lax.psum(partial_latent, ('team', 'head')).astype(jnp.bfloat16)  26 us
    dot_general x3, matrix products, compute(): jnp.einsum('kgts,skd->kgtd', weights.astype(jnp.bfloat16), block_values,...  12.1 us
    unnamed x7, local copies, waits for them, and re-layouts  7.28 us
    reduce_sum x3, other arithmetic, compute(): row_sum = row_sum * factor + jnp.sum(weights, axis=-1)  6.09 us
    dot_general x3, matrix products, compute(): jnp.einsum('tkgd,skd->kgts', query_rows, block_keys, preferred_element_ty...  4.2 us
    another operation x1, loops' own time, attend(): result, _ = lax.scan(advance, running, (key_split, value_split, pos_split))  3.67 us
  transfers between devices with their start and end apart: 2, of which 2 were waited for; matrix products, arithmetic and copies ran while one was open for 5% of the time, Pallas kernels for 0%

commit v1 on v0

--- a/solution.py
+++ b/solution.py
@@ -5,6 +5,12 @@
 from jax.sharding import PartitionSpec as P
 
 NEG_FILL = -1e30
+
+
+def rounds_take(xin):
+    for c in ("head", "team"):
+        xin = jax.lax.psum(xin, axis_name=c)
+    return xin
 
 
 def block_length(row_count):
@@ -95,7 +101,7 @@
     chosen = adapter_ids[my_block]
     down_rows = lax.dynamic_index_in_dim(adapter_down, chosen, 0, keepdims=False)
     partial_latent = jnp.dot(features, down_rows, preferred_element_type=jnp.float32)
-    latent = lax.psum(partial_latent, ("team", "head")).astype(jnp.bfloat16)
+    latent = rounds_take(partial_latent).astype(jnp.bfloat16)
 
     def expand(up_table, base_rows):
         up_rows = lax.dynamic_index_in_dim(up_table, chosen, 0, keepdims=False).reshape(

time: 161 us -> 177 us (1.099)
  waiting for transfers between devices: 65.4 us -> 97.6 us
  blocking collectives: 26 us -> 9.44 us
    psum x0 -> x1, waiting for transfers between devices: none -> 32.5 us  [rounds_take(): xin = jax.lax.psum(xin, axis_name=c)]
    psum x1, blocking collectives: 26 us -> 9.44 us  [rounds_take(): xin = jax.lax.psum(xin, axis_name=c)]
  transfers between devices with their start and end apart: 2 -> 3, of which waited for: 2 -> 3; matrix products, arithmetic and copies ran while one was open for 5% -> 6% of each run, Pallas kernels for 0% -> 0%
where the time goes in v1:
time: 177 us; the launch traced here: 176 us
  waiting for transfers between devices  97.6 us (55%)
  matrix products  20.4 us (12%)
  between operations  15.7 us (9%)
  local copies, waits for them, and re-layouts  14.8 us (8%)
  other arithmetic  14.6 us (8%)
  blocking collectives  9.44 us (5%)
  loops' own time  3.9 us (2%)
    all_gather x1, waiting for transfers between devices, on_device(): value_piece = lax.all_gather(value_rows, 'blk', axis=0, tiled=True)  36 us
    psum x1, waiting for transfers between devices, rounds_take(): xin = jax.lax.psum(xin, axis_name=c)  32.5 us
    all_gather x1, waiting for transfers between devices, on_device(): key_piece = lax.all_gather(key_rows, 'blk', axis=0, tiled=True)  29 us
    dot_general x3, matrix products, compute(): jnp.einsum('kgts,skd->kgtd', weights.astype(jnp.bfloat16), block_values,...  12.1 us
    psum x1, blocking collectives, rounds_take(): xin = jax.lax.psum(xin, axis_name=c)  9.44 us
    unnamed x7, local copies, waits for them, and re-layouts  7.28 us
    reduce_sum x3, other arithmetic, compute(): row_sum = row_sum * factor + jnp.sum(weights, axis=-1)  6.09 us
    dot_general x3, matrix products, compute(): jnp.einsum('tkgd,skd->kgts', query_rows, block_keys, preferred_element_ty...  4.2 us
  transfers between devices with their start and end apart: 3, of which 3 were waited for; matrix products, arithmetic and copies ran while one was open for 6% of the time, Pallas kernels for 0%

profile of v1, /device:TPU:0, one launch (start us, length us, event | category | flops | bytes accessed | tf_op | source)
XLA Modules:
  0.0 176.5 jit_solution(5604403744250733096)
XLA Ops:
  6.5 1.3 dynamic_slice.39
  9.8 1.8 %convolution_bitcast_fusion = f32[256,64]{0,1:T(8,128)} fusion(bf16[256,1024]{1,0:T(8,128)(2,1)S(1)} %copy-done, bf16[4,1024,64]{1,2,0:T(8,128)(2,1)} %param.17, s32[]{:T(128)S(6)} %select_n.51), kind=kOutput, calls=%fused_computation.28 | convolution fusion | flops 33554432 | bytes 720900 | tf_op jit(solution)/shard_map/dot_general | solution.py:103
  11.6 0.0 all-reduce.2.cloned.1.call-update
  11.6 0.0 all-gather.3.cloned.1.call-start
  11.7 0.8 constant_dynamic-slice_fusion.1
  12.5 1.0 copy.35
  13.5 32.5 %all-reduce.2.cloned.1.call-done = f32[256,64]{0,1:T(8,128)} async-done(((f32[256,64]{0,1:T(8,128)}), f32[256,64]{0,1:T(8,128)}) %all-reduce.2.cloned.1.call-update) | async-done | bytes 65552 | tf_op jit(solution)/shard_map/psum | solution.py:12
  46.0 9.4 %psum.15 = bf16[256,64]{0,1:T(8,128)(2,1)S(1)} all-reduce(f32[256,64]{0,1:T(8,128)} %all-reduce.2.cloned.1.call-done), channel_id=1, replica_groups=mesh['team'=2,'blk'=4,'head'=4] {'team'}, use_global_device_ids=true, to_apply=%region_1.2 | all-reduce | flops 16384 | bytes 98304 | tf_op jit(solution)/shard_map/psum | solution.py:12
  55.5 1.1 fusion.21
  56.6 0.8 pad_maximum_fusion
  57.4 0.0 all-gather.3.cloned.1.call-update
  57.4 0.0 all-gather.5.cloned.1.call-start
  57.5 1.0 copy.38
  58.4 1.1 fusion.22
  59.6 0.8 pad_maximum_fusion.1
  60.4 1.2 dynamic_slice.38
  62.2 0.6 add_reduce_fusion
  62.8 1.1 copy.40
  63.9 0.8 select_reduce_fusion
  64.8 29.0 %all-gather.3.cloned.1.call-done = bf16[3072,2,128]{2,0,1:T(8,128)(2,1)} async-done(((bf16[768,2,128]{2,0,1:T(8,128)(2,1)}), bf16[3072,2,128]{2,0,1:T(8,128)(2,1)}) %all-gather.3.cloned.1.call-update) | async-done | bytes 1572880 | tf_op jit(solution)/shard_map/all_gather | solution.py:125
  93.8 1.5 copy.39
  95.3 36.0 %all-gather.5.cloned.1.call-done = bf16[3072,2,128]{2,0,1:T(8,128)(2,1)} async-done(((bf16[768,2,128]{2,0,1:T(8,128)(2,1)}), bf16[3072,2,128]{2,0,1:T(8,128)(2,1)}) %all-gather.5.cloned.1.call-update) | async-done | bytes 1572880 | tf_op jit(solution)/shard_map/all_gather | solution.py:126
  131.3 2.7 %copy.41 = bf16[3,1024,2,128]{3,1,2,0:T(8,128)(2,1)} copy(bf16[3,1024,2,128]{3,1,0,2:T(8,128)(2,1)} %bitcast.83) | data formatting | bytes 3145728
  133.9 1.0 broadcast_in_dim.56
  135.0 31.8 %while.15 = (s32[]{:T(128)}, f32[2,4,256]{2,1,0:T(4,128)S(1)}, f32[2,4,256]{2,1,0:T(4,128)S(1)}, f32[2,4,256,128]{3,2,1,0:T(8,128)}, s32[3,1024]{1,0:T(4,128)S(1...) while((s32[]{:T(128)}, f32[2,4,256]{2,1,0:T(4,128)S(1)}, ...), condition=%wide.region_10.11_spmd.clone, body=%wide.region_4.10_spmd.clone.sunk | while | flops 1101796608 | bytes 38421312 | solution.py:75
  135.0 0.6 fusion.45
  136.9 8.7 %conditional.3 = (f32[2,4,256]{2,1,0:T(4,128)S(1)}, f32[2,4,256]{2,1,0:T(4,128)S(1)}, f32[2,4,256,128]{3,2,1,0:T(8,128)}) conditional(s32[]{:T(128)} %convert_element_type.57, (s32[1,1024]{1,0:T(1,128)S(1)}, s32[]{:T(128)}, bf16[3,1024,2,128]{3,1,2,0:T(8,128)(2,1)S(1)}, s32[]{:T(128)}, bf16[256,2,4,128]{3,0,2,1:T(8,128)(2,1)S(1)}, ...), branch_computations={%region_6.8_spmd, %region_9.9_spmd} | conditional | flops 1101795584 | bytes 38395480 | solution.py:73
  136.9 0.2 broadcast_compare_fusion
  137.1 1.4 fusion.2
  138.5 2.0 %fusion.4 = f32[2,4,256]{2,1,0:T(4,128)S(1)} fusion(f32[2,1024,256,4]{2,1,3,0:T(8,128)S(1)} %get-tuple-element.228, f32[2,4,256]{2,1,0:T(4,128)S(1)} %max.4, pred[256,1024]{0,1:T(8,128)(4,1)S(1)} %broadcast_compare_fusion), kind=kLoop, calls=%fused_computation.5 | loop fusion | flops 10483712 | bytes 8667136 | tf_op jit(solution)/shard_map/while/body/eval_jaxpr/cond/branch_0_fun/reduce_sum | solution.py:63
  140.6 4.0 %fusion.8 = f32[2,4,256,128]{3,2,1,0:T(8,128)S(1)} fusion(f32[2,1024,256,4]{2,1,3,0:T(8,128)S(1)} %get-tuple-element.228, f32[2,4,256]{2,1,0:T(4,128)S(1)} %max.4, pred[256,1024]{0,1:T(8,128)(4,1)S(1)} %broadcast_compare_fusion, f32[2,4,256,128]{3,2,1,0:T(8,128)S(1)} %copy-done.1, bf16[3,1024,2,128]{3,1,2,0:T(8,128)(2,1)} %get-tuple-element.125, ...), kind=kOutput, calls=%fused_computation.8 | convolution fusion | flops 547880960 | bytes 11289088 | tf_op jit(solution)/shard_map/while/body/eval_jaxpr/cond/branch_0_fun/kgts,skd->kgtd/dot_general | solution.py:64
  144.6 1.0 copy-done.2
  145.6 0.6 fusion.45
  147.5 8.7 %conditional.3 = (f32[2,4,256]{2,1,0:T(4,128)S(1)}, f32[2,4,256]{2,1,0:T(4,128)S(1)}, f32[2,4,256,128]{3,2,1,0:T(8,128)}) conditional(s32[]{:T(128)} %convert_element_type.57, (s32[1,1024]{1,0:T(1,128)S(1)}, s32[]{:T(128)}, bf16[3,1024,2,128]{3,1,2,0:T(8,128)(2,1)S(1)}, s32[]{:T(128)}, bf16[256,2,4,128]{3,0,2,1:T(8,128)(2,1)S(1)}, ...), branch_computations={%region_6.8_spmd, %region_9.9_spmd} | conditional | flops 1101795584 | bytes 38395480 | solution.py:73
  147.5 0.2 broadcast_compare_fusion
  147.7 1.4 fusion.2
  149.1 2.0 %fusion.4 = f32[2,4,256]{2,1,0:T(4,128)S(1)} fusion(f32[2,1024,256,4]{2,1,3,0:T(8,128)S(1)} %get-tuple-element.228, f32[2,4,256]{2,1,0:T(4,128)S(1)} %max.4, pred[256,1024]{0,1:T(8,128)(4,1)S(1)} %broadcast_compare_fusion), kind=kLoop, calls=%fused_computation.5 | loop fusion | flops 10483712 | bytes 8667136 | tf_op jit(solution)/shard_map/while/body/eval_jaxpr/cond/branch_0_fun/reduce_sum | solution.py:63
  151.2 4.0 %fusion.8 = f32[2,4,256,128]{3,2,1,0:T(8,128)S(1)} fusion(f32[2,1024,256,4]{2,1,3,0:T(8,128)S(1)} %get-tuple-element.228, f32[2,4,256]{2,1,0:T(4,128)S(1)} %max.4, pred[256,1024]{0,1:T(8,128)(4,1)S(1)} %broadcast_compare_fusion, f32[2,4,256,128]{3,2,1,0:T(8,128)S(1)} %copy-done.1, bf16[3,1024,2,128]{3,1,2,0:T(8,128)(2,1)} %get-tuple-element.125, ...), kind=kOutput, calls=%fused_computation.8 | convolution fusion | flops 547880960 | bytes 11289088 | tf_op jit(solution)/shard_map/while/body/eval_jaxpr/cond/branch_0_fun/kgts,skd->kgtd/dot_general | solution.py:64
  155.2 1.0 copy-done.2
  156.2 0.6 fusion.45
  158.1 8.7 %conditional.3 = (f32[2,4,256]{2,1,0:T(4,128)S(1)}, f32[2,4,256]{2,1,0:T(4,128)S(1)}, f32[2,4,256,128]{3,2,1,0:T(8,128)}) conditional(s32[]{:T(128)} %convert_element_type.57, (s32[1,1024]{1,0:T(1,128)S(1)}, s32[]{:T(128)}, bf16[3,1024,2,128]{3,1,2,0:T(8,128)(2,1)S(1)}, s32[]{:T(128)}, bf16[256,2,4,128]{3,0,2,1:T(8,128)(2,1)S(1)}, ...), branch_computations={%region_6.8_spmd, %region_9.9_spmd} | conditional | flops 1101795584 | bytes 38395480 | solution.py:73
  158.1 0.2 broadcast_compare_fusion
  158.3 1.4 fusion.2
  159.7 2.0 %fusion.4 = f32[2,4,256]{2,1,0:T(4,128)S(1)} fusion(f32[2,1024,256,4]{2,1,3,0:T(8,128)S(1)} %get-tuple-element.228, f32[2,4,256]{2,1,0:T(4,128)S(1)} %max.4, pred[256,1024]{0,1:T(8,128)(4,1)S(1)} %broadcast_compare_fusion), kind=kLoop, calls=%fused_computation.5 | loop fusion | flops 10483712 | bytes 8667136 | tf_op jit(solution)/shard_map/while/body/eval_jaxpr/cond/branch_0_fun/reduce_sum | solution.py:63
  161.8 4.0 %fusion.8 = f32[2,4,256,128]{3,2,1,0:T(8,128)S(1)} fusion(f32[2,1024,256,4]{2,1,3,0:T(8,128)S(1)} %get-tuple-element.228, f32[2,4,256]{2,1,0:T(4,128)S(1)} %max.4, pred[256,1024]{0,1:T(8,128)(4,1)S(1)} %broadcast_compare_fusion, f32[2,4,256,128]{3,2,1,0:T(8,128)S(1)} %copy-done.1, bf16[3,1024,2,128]{3,1,2,0:T(8,128)(2,1)} %get-tuple-element.125, ...), kind=kOutput, calls=%fused_computation.8 | convolution fusion | flops 547880960 | bytes 11289088 | tf_op jit(solution)/shard_map/while/body/eval_jaxpr/cond/branch_0_fun/kgts,skd->kgtd/dot_general | solution.py:64
  165.8 1.0 copy-done.2
  166.8 0.2 copy.42
  167.0 2.9 %fusion.24 = bf16[256,2,4,128]{3,2,1,0:T(4,128)(2,1)} fusion(f32[2,4,256]{1,0,2:T(2,128)S(1)} %copy.42, f32[2,4,256,128]{3,2,1,0:T(8,128)} %get-tuple-element.142), kind=kLoop, calls=%fused_computation.31 | loop fusion | flops 524288 | bytes 1581056 | tf_op jit(solution)/shard_map/convert_element_type | solution.py:134
  (34 shorter events, 0.2 us)
Async XLA Ops:
  6.5 3.2 %copy-start = (bf16[256,1024]{1,0:T(8,128)(2,1)S(1)}, bf16[256,1024]{1,0:T(8,128)(2,1)}, u32[]{:S(2)}) copy-start(bf16[256,1024]{1,0:T(8,128)(2,1)} %param.16) | copy-start | bytes 1572868
  6.5 39.5 %all-reduce.2.cloned.1.call-start = ((), (), s32[]{:S(2)}) async-start(), calls=%async_computation | async-start | bytes 131072 | tf_op jit(solution)/shard_map/psum | solution.py:12
  11.6 82.1 %all-gather.3.cloned.1.call-start = ((), (), s32[]{:S(2)}) async-start(), calls=%async_computation.1 | async-start | bytes 1966080 | tf_op jit(solution)/shard_map/all_gather | solution.py:125
  57.4 73.9 %all-gather.5.cloned.1.call-start = ((), (), s32[]{:S(2)}) async-start(), calls=%async_computation.2 | async-start | bytes 1966080 | tf_op jit(solution)/shard_map/all_gather | solution.py:126
  137.1 3.5 %copy-start.1 = (f32[2,4,256,128]{3,2,1,0:T(8,128)S(1)}, f32[2,4,256,128]{3,2,1,0:T(8,128)}, u32[]{:S(2)}) copy-start(f32[2,4,256,128]{3,2,1,0:T(8,128)} %get-tuple-element.124) | copy-start | bytes 3145732 | tf_op jit(solution)/shard_map/while/body/eval_jaxpr/cond
  144.6 1.0 copy-start.2
  147.7 3.5 %copy-start.1 = (f32[2,4,256,128]{3,2,1,0:T(8,128)S(1)}, f32[2,4,256,128]{3,2,1,0:T(8,128)}, u32[]{:S(2)}) copy-start(f32[2,4,256,128]{3,2,1,0:T(8,128)} %get-tuple-element.124) | copy-start | bytes 3145732 | tf_op jit(solution)/shard_map/while/body/eval_jaxpr/cond
  155.2 1.0 copy-start.2
  158.3 3.5 %copy-start.1 = (f32[2,4,256,128]{3,2,1,0:T(8,128)S(1)}, f32[2,4,256,128]{3,2,1,0:T(8,128)}, u32[]{:S(2)}) copy-start(f32[2,4,256,128]{3,2,1,0:T(8,128)} %get-tuple-element.124) | copy-start | bytes 3145732 | tf_op jit(solution)/shard_map/while/body/eval_jaxpr/cond
  165.8 1.0 copy-start.2
Sparse Core Ops, SparseCore 0:
  11.8 34.2 all-reduce.1
  57.5 36.1 all-gather.2
  95.3 35.8 all-gather.4
